TPU v7x, 256 devices: a whole 4x4x8 slice. The times are simulated.
256 devices in a mesh: row: 16 (over y_lo, z), col: 16 (over x, y_hi, core).
Axes of the slice: x: 4, y: 4 (y_hi: 2, y_lo: 2; y = y_hi * 2 + y_lo), z: 8, core: 2. Of those that a mesh axis runs over, the one named last changes fastest.
Arguments:
- object_field: float32 [2, 2, 4096, 4096], P(None, None, 'row', 'col'), may hold values from -4 to 4
- probe: float32 [2, 128, 128], replicated, may hold values from -6 to 6
- intensity: float32 [16, 128, 128, 128], P('row', 'col'), may hold values from 0 to 2
- offset_row: int32 [16, 128], P('row', 'col'), may hold values from 0 to 255
- offset_col: int32 [16, 128], P('row', 'col'), may hold values from 0 to 255
- live: int32 [16, 16], P('row', 'col'), may hold values from 1 to 8, as said below
Outputs:
- new_object: float32 [2, 2, 4096, 4096], P(None, None, 'row', 'col')
- new_probe: float32 [2, 128, 128], replicated
Inputs may be any that keep to these rules, and one draw needn't show every extreme that they name: Device (a, b) uses its first live[a, b] slots; at least one device uses all 8.
All inputs are finite; a program needn't handle non-finite values.
Results may differ from a plain program's by a relative error of at most 0.0003.
Values sent between devices are 32-bit elements; how exact they have to be, the bound alone decides.
No kernel may reach another device: no remote copies, remote signals or barrier semaphores. Data moves between devices by JAX's collectives and lax.ppermute only.
A program may use at most 64 MiB of HBM per device.

v0:
```python
import math
import jax
import jax.numpy as jnp
from jax import lax
from jax.sharding import PartitionSpec as P

STEP_OBJECT = 0.03
STEP_PROBE = 2.0
FRESNEL_PHASE = 60.0


def with_halo(block, sides, width):
    for axis, dim in sides:
        count = lax.axis_size(axis)
        forward = [(i, i + 1) for i in range(count - 1)]
        backward = [(target, source) for source, target in forward]
        low = lax.ppermute(
            lax.slice_in_dim(block, block.shape[dim] - width, None, axis=dim), axis, forward
        )
        high = lax.ppermute(lax.slice_in_dim(block, 0, width, axis=dim), axis, backward)
        block = jnp.concatenate([low, block, high], axis=dim)
    return block


def make_tables(width):
    index = jnp.arange(width, dtype=jnp.int32)
    product = index[:, None] * index[None, :] % width
    angle = 2.0 * math.pi / width * product.astype(jnp.float32)
    scale = 1.0 / math.sqrt(width)
    four_re = jnp.cos(angle) * scale
    four_im = -jnp.sin(angle) * scale
    freq = jnp.where(index < width // 2, index, index - width).astype(jnp.float32) / width
    phase = -FRESNEL_PHASE * (freq[:, None] ** 2 + freq[None, :] ** 2)
    return (four_re, four_im, jnp.cos(phase), jnp.sin(phase))


def transform(wave_re, wave_im, four_re, four_im):
    high = lax.Precision.HIGHEST
    right_re = jnp.einsum("kab,bc->kac", wave_re, four_re, precision=high) - jnp.einsum(
        "kab,bc->kac", wave_im, four_im, precision=high
    )
    right_im = jnp.einsum("kab,bc->kac", wave_re, four_im, precision=high) + jnp.einsum(
        "kab,bc->kac", wave_im, four_re, precision=high
    )
    out_re = jnp.einsum("ab,kbc->kac", four_re, right_re, precision=high) - jnp.einsum(
        "ab,kbc->kac", four_im, right_im, precision=high
    )
    out_im = jnp.einsum("ab,kbc->kac", four_im, right_re, precision=high) + jnp.einsum(
        "ab,kbc->kac", four_re, right_im, precision=high
    )
    return (out_re, out_im)


def window_grads(windows, probe, measured, active, tabs):
    four_re, four_im, prop_re, prop_im = tabs
    probe_re, probe_im = (probe[0], probe[1])
    first_re, first_im = (windows[:, 0, 0], windows[:, 0, 1])
    second_re, second_im = (windows[:, 1, 0], windows[:, 1, 1])
    wave_re = probe_re * first_re - probe_im * first_im
    wave_im = probe_re * first_im + probe_im * first_re
    spec_re, spec_im = transform(wave_re, wave_im, four_re, four_im)
    spec_re, spec_im = (
        spec_re * prop_re - spec_im * prop_im,
        spec_re * prop_im + spec_im * prop_re,
    )
    mid_re, mid_im = transform(spec_re, spec_im, four_re, -four_im)
    exit_re = mid_re * second_re - mid_im * second_im
    exit_im = mid_re * second_im + mid_im * second_re
    far_re, far_im = transform(exit_re, exit_im, four_re, four_im)
    weight = 2.0 * (far_re * far_re + far_im * far_im - measured) * active[:, None, None]
    chi_re, chi_im = transform(weight * far_re, weight * far_im, four_re, -four_im)
    back_re = second_re * chi_re + second_im * chi_im
    back_im = second_re * chi_im - second_im * chi_re
    grad2_re = mid_re * chi_re + mid_im * chi_im
    grad2_im = mid_re * chi_im - mid_im * chi_re
    spec_re, spec_im = transform(back_re, back_im, four_re, four_im)
    spec_re, spec_im = (
        spec_re * prop_re + spec_im * prop_im,
        spec_im * prop_re - spec_re * prop_im,
    )
    down_re, down_im = transform(spec_re, spec_im, four_re, -four_im)
    grad1_re = probe_re * down_re + probe_im * down_im
    grad1_im = probe_re * down_im - probe_im * down_re
    probe_gre = jnp.sum(first_re * down_re + first_im * down_im, axis=0)
    probe_gim = jnp.sum(first_re * down_im - first_im * down_re, axis=0)
    grads = jnp.stack([jnp.stack([grad1_re, grad1_im], 1), jnp.stack([grad2_re, grad2_im], 1)], 1)
    return (grads, jnp.stack([probe_gre, probe_gim]))


def squeeze_rim(grid, axis, half, tile):
    width = 2 * half
    return jnp.concatenate(
        [
            lax.slice_in_dim(grid, 0, half, axis=axis),
            lax.slice_in_dim(grid, width, tile, axis=axis),
            lax.slice_in_dim(grid, tile + half, tile + width, axis=axis),
        ],
        axis=axis,
    )


def on_device(object_field, probe, intensity, offset_row, offset_col, live):
    tile = object_field.shape[2]
    width = probe.shape[1]
    half = width // 2
    slot_count = offset_row.shape[1]
    extended = with_halo(object_field, (("row", 2), ("col", 3)), half)
    row_start = offset_row[0]
    col_start = offset_col[0]
    active = (jnp.arange(slot_count, dtype=jnp.int32) < live[0, 0]).astype(jnp.float32)
    windows = jax.vmap(
        lambda rstart, cstart: lax.dynamic_slice(
            extended, (jnp.int32(0), jnp.int32(0), rstart, cstart), (2, 2, width, width)
        )
    )(row_start, col_start)
    grads, probe_part = window_grads(windows, probe, intensity[0], active, make_tables(width))

    def add_slot(slot, accum_grad):
        start = (jnp.int32(0), jnp.int32(0), row_start[slot], col_start[slot])
        current = lax.dynamic_slice(accum_grad, start, (2, 2, width, width))
        return lax.dynamic_update_slice(accum_grad, current + grads[slot], start)

    grad_ext = lax.fori_loop(0, slot_count, add_slot, jnp.zeros(extended.shape, jnp.float32))
    row_set = squeeze_rim(grad_ext[:, :, :, half : tile + half], 2, half, tile)
    col_set = squeeze_rim(grad_ext[:, :, half : tile + half, :], 3, half, tile)
    corner_set = squeeze_rim(squeeze_rim(grad_ext, 2, half, tile), 3, half, tile)
    packed = jnp.concatenate([row_set, col_set, corner_set], axis=0)
    returned = with_halo(packed, (("row", 2), ("col", 3)), half)
    from_rows = returned[0:2]
    from_cols = returned[2:4]
    from_corner = returned[4:6]
    inner = grad_ext[:, :, half : tile + half, half : tile + half]
    inner = inner.at[:, :, :half, :].add(from_rows[:, :, :half, half : tile + half])
    inner = inner.at[:, :, tile - half :, :].add(from_rows[:, :, tile + half :, half : tile + half])
    inner = inner.at[:, :, :, :half].add(from_cols[:, :, half : tile + half, :half])
    inner = inner.at[:, :, :, tile - half :].add(from_cols[:, :, half : tile + half, tile + half :])
    inner = inner.at[:, :, :half, :half].add(from_corner[:, :, :half, :half])
    inner = inner.at[:, :, :half, tile - half :].add(from_corner[:, :, :half, tile + half :])
    inner = inner.at[:, :, tile - half :, :half].add(from_corner[:, :, tile + half :, :half])
    inner = inner.at[:, :, tile - half :, tile - half :].add(
        from_corner[:, :, tile + half :, tile + half :]
    )
    probe_total = lax.psum(probe_part, ("row", "col"))
    count_all = slot_count * lax.axis_size("row") * lax.axis_size("col")
    new_object = object_field - STEP_OBJECT * inner
    new_probe = probe - STEP_PROBE / count_all * probe_total
    return (new_object, new_probe)


def solution(mesh):
    placed = (
        P(None, None, "row", "col"),
        P(),
        P("row", "col", None, None),
        P("row", "col"),
        P("row", "col"),
        P("row", "col"),
    )
    return jax.shard_map(
        on_device,
        mesh=mesh,
        in_specs=placed,
        out_specs=(P(None, None, "row", "col"), P()),
        check_vma=False,
    )
```

profile of v0, /device:TPU:8, one launch (start us, length us, event | category | flops | bytes accessed | tf_op | source)
XLA Modules:
  0.0 537.3 jit_solution(3753956804749507980)
XLA Ops:
  9.0 7.6 %collective-permute-start.1 = (f32[2,2,64,256]{2,3,1,0:T(8,128)S(1)}, f32[2,2,64,256]{2,3,1,0:T(8,128)S(1)}, u32[]{:S(2)}, u32[]{:S(2)}) collective-permute-start(f32[2,2,64,256]{2,3,1,0:T(8,128)S(1)} %get-tuple-element.283), channel_id=1, source_target_pairs={{16,0},{32,16},{48,32},{64,48},{80,64},{96,80},{112,96},{128,112},... | collective-permute-start | bytes 786440 | tf_op jit(solution)/shard_map/ppermute | solution.py:20
  18.8 9.1 %collective-permute-done.1 = f32[2,2,64,256]{2,3,1,0:T(8,128)S(1)} collective-permute-done((f32[2,2,64,256]{2,3,1,0:T(8,128)S(1)}, f32[2,2,64,256]{2,3,1,0:T(8,128)S(1)}, u32[]{:S(2)}, u32[]{:S(2)}) %collective-permute-start.1) | collective-permute-done | bytes 262176 | tf_op jit(solution)/shard_map/ppermute | solution.py:20
  27.9 6.5 %collective-permute-done = f32[2,2,64,256]{2,3,1,0:T(8,128)S(1)} collective-permute-done((f32[2,2,64,256]{2,3,1,0:T(8,128)S(1)}, f32[2,2,64,256]{2,3,1,0:T(8,128)S(1)}, u32[]{:S(2)}, u32[]{:S(2)}) %collective-permute-start) | collective-permute-done | bytes 262176 | tf_op jit(solution)/shard_map/ppermute | solution.py:17
  36.9 3.8 collective-permute-start.2
  43.9 3.5 pad_maximum_fusion.1
  47.4 27.8 %while.23 = (s32[]{:T(128)}, f32[2,2,384,384]{2,3,1,0:T(8,128)}, s32[8,4]{0,1:T(4,128)S(1)}, f32[8,2,2,128,128]{3,4,0,2,1:T(8,128)S(1)}, s32[]{:T(128)}) while((s32[]{:T(128)}, f32[2,2,384,384]{2,3,1,0:T(8,128)}, s32[8,4]{0,1:T(4,128)S(1)}, f32[8,2,2,128,128]{3,4,0,2,1:T(8,128)S(1)}, s32[]{:T(128)}) %tuple.110), condition=%wide.while_cond.8, body=%wide.while_body.8.sunk | while | flops 2 | bytes 2097285 | solution.py:112
  48.0 2.4 constant_dynamic-slice_fusion.8
  51.4 2.4 constant_dynamic-slice_fusion.8
  54.8 2.4 constant_dynamic-slice_fusion.8
  58.3 2.4 constant_dynamic-slice_fusion.8
  61.7 2.4 constant_dynamic-slice_fusion.8
  65.1 2.4 constant_dynamic-slice_fusion.8
  68.5 2.4 constant_dynamic-slice_fusion.8
  71.9 2.4 constant_dynamic-slice_fusion.8
  133.5 77.9 %while.22 = (s32[]{:T(128)}, f32[2,2,384,384]{3,2,1,0:T(8,128)S(1)}, s32[8]{0:T(128)S(1)}, s32[8]{0:T(128)S(1)}, f32[8,2,2,128,128]{3,4,0,2,1:T(8,128)}, /*index=5*/s32[]{:T(128)}, s32[]{:T(128)}, s32[]{:T(128)}) while((s32[]{:T(128)}, f32[2,2,384,384]{3,2,1,0:T(8,128)S(1)}, s32[8]{0:T(128)S(1)}, s32[8]{0:T(128)S(1)}, ...), condition=%wide.region_1.2_spmd, body=%wide.region_0.1_spmd.sunk | while | flops 65544 | bytes 2359497 | solution.py:123
  139.9 3.2 dynamic_update_slice.8
  149.4 3.1 dynamic_update_slice.8
  158.9 3.4 dynamic_update_slice.8
  168.7 3.4 dynamic_update_slice.8
  178.4 3.4 dynamic_update_slice.8
  188.2 3.4 dynamic_update_slice.8
  198.0 3.4 dynamic_update_slice.8
  207.8 3.4 dynamic_update_slice.8
  214.9 6.0 %collective-permute-start.5 = (f32[6,2,64,256]{3,2,1,0:T(8,128)S(1)}, f32[6,2,64,256]{3,2,1,0:T(8,128)S(1)}, u32[]{:S(2)}, u32[]{:S(2)}) collective-permute-start(f32[6,2,64,256]{3,2,1,0:T(8,128)S(1)} %get-tuple-element.252), channel_id=1, source_target_pairs={{16,0},{32,16},{48,32},{64,48},{80,64},{96,80},{112,96},{128,112},... | collective-permute-start | bytes 2359304 | tf_op jit(solution)/shard_map/ppermute | solution.py:20
  221.0 12.3 %collective-permute-done.4 = f32[6,2,64,256]{3,2,1,0:T(8,128)S(1)} collective-permute-done((f32[6,2,64,256]{3,2,1,0:T(8,128)S(1)}, f32[6,2,64,256]{3,2,1,0:T(8,128)S(1)}, u32[]{:S(2)}, u32[]{:S(2)}) %collective-permute-start.4) | collective-permute-done | bytes 786464 | tf_op jit(solution)/shard_map/ppermute | solution.py:17
  237.3 2.9 fusion.370
  240.3 2.8 copy.199
  243.1 6.9 %collective-permute-start.6 = (f32[6,2,384,64]{2,3,1,0:T(8,128)}, f32[6,2,384,64]{2,3,1,0:T(8,128)}, u32[]{:S(2)}, u32[]{:S(2)}) collective-permute-start(f32[6,2,384,64]{2,3,1,0:T(8,128)} %copy.199), channel_id=1, source_target_pairs={{0,1},{1,2},{2,3},{3,4},{4,5},{5,6},{6,7},{7,8},{8,9},{9,10},{10,1... | collective-permute-start | bytes 3538952 | tf_op jit(solution)/shard_map/ppermute | solution.py:17
  250.8 2.8 copy.201
  256.6 247.3 %all-reduce.2.cloned.1.call-done = f32[2,128,128]{1,2,0:T(8,128)} async-done(((f32[2,128,128]{1,2,0:T(8,128)}), f32[2,128,128]{1,2,0:T(8,128)}) %all-reduce.2.cloned.1.call-update) | async-done | bytes 131088 | tf_op jit(solution)/shard_map/psum | solution.py:143
  515.6 2.4 scatter-add.31
  522.3 3.5 scatter-add.35
  (222 shorter events, 125.4 us)
Async XLA Ops:
  7.2 11.5 %copy-start.8 = (s32[1,8]{1,0:T(1,128)S(1)}, s32[1,8]{1,0:T(1,128)}, u32[]{:S(2)}) copy-start(s32[1,8]{1,0:T(1,128)} %param.27) | copy-start | bytes 100
  7.2 11.5 %copy-start.9 = (s32[1,8]{1,0:T(1,128)S(1)}, s32[1,8]{1,0:T(1,128)}, u32[]{:S(2)}) copy-start(s32[1,8]{1,0:T(1,128)} %param.28) | copy-start | bytes 100
  7.2 11.6 %copy-start.6 = (f32[2,128,128]{2,1,0:T(8,128)S(1)}, f32[2,128,128]{2,1,0:T(8,128)}, u32[]{:S(2)}) copy-start(f32[2,128,128]{2,1,0:T(8,128)} %param.25) | copy-start | bytes 393220
  7.2 496.6 %all-reduce.2.cloned.1.call-start = ((), (), s32[]{:S(2)}) async-start(), calls=%async_computation | async-start | bytes 262144 | tf_op jit(solution)/shard_map/psum | solution.py:143
  9.0 18.8 %collective-permute-start.1 = (f32[2,2,64,256]{2,3,1,0:T(8,128)S(1)}, f32[2,2,64,256]{2,3,1,0:T(8,128)S(1)}, u32[]{:S(2)}, u32[]{:S(2)}) collective-permute-start(f32[2,2,64,256]{2,3,1,0:T(8,128)S(1)} %get-tuple-element.283), channel_id=1, source_target_pairs={{16,0},{32,16},{48,32},{64,48},{80,64},{96,80},{112,96},{128,112},... | collective-permute-start | bytes 786440 | tf_op jit(solution)/shard_map/ppermute | solution.py:20
  16.7 17.6 %collective-permute-start = (f32[2,2,64,256]{2,3,1,0:T(8,128)S(1)}, f32[2,2,64,256]{2,3,1,0:T(8,128)S(1)}, u32[]{:S(2)}, u32[]{:S(2)}) collective-permute-start(f32[2,2,64,256]{2,3,1,0:T(8,128)S(1)} %get-tuple-element.282), channel_id=1, source_target_pairs={{0,16},{16,32},{32,48},{48,64},{64,80},{80,96},{96,112},{112,128},... | collective-permute-start | bytes 786440 | tf_op jit(solution)/shard_map/ppermute | solution.py:17
  27.9 6.5 %copy-start.1 = (f32[2,2,64,256]{2,3,1,0:T(8,128)}, f32[2,2,64,256]{2,3,1,0:T(8,128)S(1)}, u32[]{:S(2)}) copy-start(f32[2,2,64,256]{2,3,1,0:T(8,128)S(1)} %collective-permute-done.1) | copy-start | bytes 786436
  34.3 1.2 copy-start.2
  35.6 8.3 %collective-permute-start.3 = (f32[2,2,384,64]{2,3,1,0:T(8,128)}, f32[2,2,384,64]{2,3,1,0:T(8,128)}, u32[]{:S(2)}, u32[]{:S(2)}) collective-permute-start(f32[2,2,384,64]{2,3,1,0:T(8,128)} %get-tuple-element.267), channel_id=1, source_target_pairs={{1,0},{2,1},{3,2},{4,3},{5,4},{6,5},{7,6},{8,7},{9,8},{10,9},{11,1... | collective-permute-start | bytes 1179656 | tf_op jit(solution)/shard_map/ppermute | solution.py:20
  36.9 7.0 %collective-permute-start.2 = (f32[2,2,384,64]{2,3,1,0:T(8,128)}, f32[2,2,384,64]{2,3,1,0:T(8,128)}, u32[]{:S(2)}, u32[]{:S(2)}) collective-permute-start(f32[2,2,384,64]{2,3,1,0:T(8,128)} %get-tuple-element.266), channel_id=1, source_target_pairs={{0,1},{1,2},{2,3},{3,4},{4,5},{5,6},{6,7},{7,8},{8,9},{9,10},{10,1... | collective-permute-start | bytes 1179656 | tf_op jit(solution)/shard_map/ppermute | solution.py:17
  97.5 4.8 copy-start.3
  213.0 20.3 %collective-permute-start.4 = (f32[6,2,64,256]{3,2,1,0:T(8,128)S(1)}, f32[6,2,64,256]{3,2,1,0:T(8,128)S(1)}, u32[]{:S(2)}, u32[]{:S(2)}) collective-permute-start(f32[6,2,64,256]{3,2,1,0:T(8,128)S(1)} %get-tuple-element.253), channel_id=1, source_target_pairs={{0,16},{16,32},{32,48},{48,64},{64,80},{80,96},{96,112},{112,128},... | collective-permute-start | bytes 2359304 | tf_op jit(solution)/shard_map/ppermute | solution.py:17
  214.9 20.1 %collective-permute-start.5 = (f32[6,2,64,256]{3,2,1,0:T(8,128)S(1)}, f32[6,2,64,256]{3,2,1,0:T(8,128)S(1)}, u32[]{:S(2)}, u32[]{:S(2)}) collective-permute-start(f32[6,2,64,256]{3,2,1,0:T(8,128)S(1)} %get-tuple-element.252), channel_id=1, source_target_pairs={{16,0},{32,16},{48,32},{64,48},{80,64},{96,80},{112,96},{128,112},... | collective-permute-start | bytes 2359304 | tf_op jit(solution)/shard_map/ppermute | solution.py:20
  233.3 4.0 copy-start.4
  235.1 2.3 copy-start.5
  240.3 9.7 %copy-start.7 = (f32[2,128,128]{2,1,0:T(8,128)S(1)}, f32[2,128,128]{2,1,0:T(8,128)}, u32[]{:S(2)}) copy-start(f32[2,128,128]{2,1,0:T(8,128)} %param.25) | copy-start | bytes 393220
  240.3 9.8 %copy-start.10 = (s32[4]{0:T(128)S(1)}, s32[4]{0:T(128)}, u32[]{:S(2)}) copy-start(s32[4]{0:T(128)} %constant.288.clone.1) | copy-start | bytes 52
  243.1 266.0 %collective-permute-start.6 = (f32[6,2,384,64]{2,3,1,0:T(8,128)}, f32[6,2,384,64]{2,3,1,0:T(8,128)}, u32[]{:S(2)}, u32[]{:S(2)}) collective-permute-start(f32[6,2,384,64]{2,3,1,0:T(8,128)} %copy.199), channel_id=1, source_target_pairs={{0,1},{1,2},{2,3},{3,4},{4,5},{5,6},{6,7},{7,8},{8,9},{9,10},{10,1... | collective-permute-start | bytes 3538952 | tf_op jit(solution)/shard_map/ppermute | solution.py:17
  253.6 259.2 %collective-permute-start.7 = (f32[6,2,384,64]{2,3,1,0:T(8,128)}, f32[6,2,384,64]{2,3,1,0:T(8,128)}, u32[]{:S(2)}, u32[]{:S(2)}) collective-permute-start(f32[6,2,384,64]{2,3,1,0:T(8,128)} %copy.201), channel_id=1, source_target_pairs={{1,0},{2,1},{3,2},{4,3},{5,4},{6,5},{7,6},{8,7},{9,8},{10,9},{11,1... | collective-permute-start | bytes 3538952 | tf_op jit(solution)/shard_map/ppermute | solution.py:20
  515.6 13.5 %copy-start = (f32[2,2,256,256]{3,2,1,0:T(8,128)S(1)}, f32[2,2,256,256]{3,2,1,0:T(8,128)}, u32[]{:S(2)}) copy-start(f32[2,2,256,256]{3,2,1,0:T(8,128)} %param.24) | copy-start | bytes 3145732
Sparse Core Ops, SparseCore 0:
  255.7 248.0 all-reduce.1
where the time goes:
time: 542 us; the launch traced here: 537 us
  waiting for transfers between devices  277 us (51%)
  local copies, waits for them, and re-layouts  106 us (20%)
  matrix products  56.2 us (10%)
  loops' own time  32.5 us (6%)
  starting transfers between devices  30.8 us (6%)
  other arithmetic  19.2 us (4%)
  between operations  15.8 us (3%)
    psum x1, waiting for transfers between devices, on_device(): probe_total = lax.psum(probe_part, ('row', 'col'))  247 us
    another operation x1, loops' own time, on_device(): lax.fori_loop(0, slot_count, add_slot, jnp.zeros(extended.shape, jnp.floa...  31.7 us
    gather x48, local copies, waits for them, and re-layouts  27 us
    dynamic_update_slice x8, local copies, waits for them, and re-layouts, add_slot(): return lax.dynamic_update_slice(accum_grad, current + grads[slot], start)  26.8 us
    ppermute x4, waiting for transfers between devices, with_halo(): lax.ppermute(lax.slice_in_dim(block, block.shape[dim] - width, None, axis...  18.8 us
    ppermute x4, starting transfers between devices, with_halo(): lax.ppermute(lax.slice_in_dim(block, 0, width, axis=dim), axis, backward)  16.2 us
    ppermute x4, starting transfers between devices, with_halo(): lax.ppermute(lax.slice_in_dim(block, block.shape[dim] - width, None, axis...  14.5 us
  transfers between devices with their start and end apart: 9, of which 5 were waited for; matrix products, arithmetic and copies ran while one was open for 3% of the time, Pallas kernels for 0%

commit v1 on v0

--- a/solution.py
+++ b/solution.py
@@ -3,10 +3,16 @@
 import jax.numpy as jnp
 from jax import lax
 from jax.sharding import PartitionSpec as P
+from jax.lax import all_gather
 
 STEP_OBJECT = 0.03
 STEP_PROBE = 2.0
 FRESNEL_PHASE = 60.0
+
+
+def settle_sites(block_in):
+    out_arr = all_gather(block_in, axis_name=("row", "col")).sum(axis=0)
+    return out_arr
 
 
 def with_halo(block, sides, width):
@@ -140,7 +146,7 @@
     inner = inner.at[:, :, tile - half :, tile - half :].add(
         from_corner[:, :, tile + half :, tile + half :]
     )
-    probe_total = lax.psum(probe_part, ("row", "col"))
+    probe_total = settle_sites(probe_part)
     count_all = slot_count * lax.axis_size("row") * lax.axis_size("col")
     new_object = object_field - STEP_OBJECT * inner
     new_probe = probe - STEP_PROBE / count_all * probe_total

time: 542 us -> 651 us (1.20)
  waiting for transfers between devices: 277 us -> 371 us
  other arithmetic: 19.2 us -> 31.5 us
    all_gather x0 -> x1, waiting for transfers between devices: none -> 333 us  [settle_sites(): out_arr = all_gather(block_in, axis_name=('row', 'col')).sum(axis=0)]
    psum x1 -> x0, waiting for transfers between devices: 247 us -> none  [on_device(): probe_total = lax.psum(probe_part, ('row', 'col'))]
    reduce_sum x0 -> x1, other arithmetic: none -> 12.2 us  [settle_sites(): out_arr = all_gather(block_in, axis_name=('row', 'col')).sum(axis=0)]
  transfers between devices with their start and end apart: 9 -> 9, of which waited for: 5 -> 5; matrix products, arithmetic and copies ran while one was open for 3% -> 14% of each run, Pallas kernels for 0% -> 0%
where the time goes in v1:
time: 651 us; the launch traced here: 642 us
  waiting for transfers between devices  371 us (57%)
  local copies, waits for them, and re-layouts  105 us (16%)
  matrix products  58.2 us (9%)
  loops' own time  32.5 us (5%)
  other arithmetic  31.5 us (5%)
  starting transfers between devices  28.3 us (4%)
  between operations  15.8 us (2%)
    all_gather x1, waiting for transfers between devices, settle_sites(): out_arr = all_gather(block_in, axis_name=('row', 'col')).sum(axis=0)  333 us
    another operation x1, loops' own time, on_device(): lax.fori_loop(0, slot_count, add_slot, jnp.zeros(extended.shape, jnp.floa...  31.7 us
    dynamic_update_slice x8, local copies, waits for them, and re-layouts, add_slot(): return lax.dynamic_update_slice(accum_grad, current + grads[slot], start)  26.8 us
    gather x48, local copies, waits for them, and re-layouts  26.4 us
    ppermute x4, waiting for transfers between devices, with_halo(): lax.ppermute(lax.slice_in_dim(block, block.shape[dim] - width, None, axis...  23.8 us
    ppermute x4, starting transfers between devices, with_halo(): lax.ppermute(lax.slice_in_dim(block, 0, width, axis=dim), axis, backward)  16.2 us
    ppermute x4, waiting for transfers between devices, with_halo(): lax.ppermute(lax.slice_in_dim(block, 0, width, axis=dim), axis, backward)  13.9 us
  transfers between devices with their start and end apart: 9, of which 5 were waited for; matrix products, arithmetic and copies ran while one was open for 14% of the time, Pallas kernels for 0%

profile of v1, /device:TPU:8, one launch (start us, length us, event | category | flops | bytes accessed | tf_op | source)
XLA Modules:
  0.0 641.8 jit_solution(11726159215069737888)
XLA Ops:
  9.0 7.6 %collective-permute-start.1 = (f32[2,2,64,256]{2,3,1,0:T(8,128)S(1)}, f32[2,2,64,256]{2,3,1,0:T(8,128)S(1)}, u32[]{:S(2)}, u32[]{:S(2)}) collective-permute-start(f32[2,2,64,256]{2,3,1,0:T(8,128)S(1)} %get-tuple-element.281), channel_id=1, source_target_pairs={{16,0},{32,16},{48,32},{64,48},{80,64},{96,80},{112,96},{128,112},... | collective-permute-start | bytes 786440 | tf_op jit(solution)/shard_map/ppermute | solution.py:26
  18.8 9.1 %collective-permute-done.1 = f32[2,2,64,256]{2,3,1,0:T(8,128)S(1)} collective-permute-done((f32[2,2,64,256]{2,3,1,0:T(8,128)S(1)}, f32[2,2,64,256]{2,3,1,0:T(8,128)S(1)}, u32[]{:S(2)}, u32[]{:S(2)}) %collective-permute-start.1) | collective-permute-done | bytes 262176 | tf_op jit(solution)/shard_map/ppermute | solution.py:26
  27.9 6.5 %collective-permute-done = f32[2,2,64,256]{2,3,1,0:T(8,128)S(1)} collective-permute-done((f32[2,2,64,256]{2,3,1,0:T(8,128)S(1)}, f32[2,2,64,256]{2,3,1,0:T(8,128)S(1)}, u32[]{:S(2)}, u32[]{:S(2)}) %collective-permute-start) | collective-permute-done | bytes 262176 | tf_op jit(solution)/shard_map/ppermute | solution.py:23
  36.9 3.8 collective-permute-start.2
  44.4 3.5 pad_maximum_fusion.1
  47.9 27.2 %while.23 = (s32[]{:T(128)}, f32[2,2,384,384]{2,3,1,0:T(8,128)}, s32[8,4]{0,1:T(4,128)S(1)}, f32[8,2,2,128,128]{3,4,0,2,1:T(8,128)S(1)}, s32[]{:T(128)}) while((s32[]{:T(128)}, f32[2,2,384,384]{2,3,1,0:T(8,128)}, s32[8,4]{0,1:T(4,128)S(1)}, f32[8,2,2,128,128]{3,4,0,2,1:T(8,128)S(1)}, s32[]{:T(128)}) %tuple.109), condition=%wide.while_cond.8, body=%wide.while_body.8.sunk | while | flops 2 | bytes 2097285 | solution.py:118
  48.5 2.4 constant_dynamic-slice_fusion.8
  51.8 2.4 constant_dynamic-slice_fusion.8
  55.2 2.4 constant_dynamic-slice_fusion.8
  58.5 2.4 constant_dynamic-slice_fusion.8
  65.2 2.4 constant_dynamic-slice_fusion.8
  68.5 2.4 constant_dynamic-slice_fusion.8
  71.9 2.4 constant_dynamic-slice_fusion.8
  137.3 77.9 %while.22 = (s32[]{:T(128)}, f32[2,2,384,384]{3,2,1,0:T(8,128)S(1)}, s32[8]{0:T(128)S(1)}, s32[8]{0:T(128)S(1)}, f32[8,2,2,128,128]{3,4,0,2,1:T(8,128)}, /*index=5*/s32[]{:T(128)}, s32[]{:T(128)}, s32[]{:T(128)}) while((s32[]{:T(128)}, f32[2,2,384,384]{3,2,1,0:T(8,128)S(1)}, s32[8]{0:T(128)S(1)}, s32[8]{0:T(128)S(1)}, ...), condition=%wide.region_1.2_spmd, body=%wide.region_0.1_spmd.sunk | while | flops 65544 | bytes 2359497 | solution.py:129
  143.6 3.2 dynamic_update_slice.8
  153.2 3.1 dynamic_update_slice.8
  162.6 3.4 dynamic_update_slice.8
  172.4 3.4 dynamic_update_slice.8
  182.2 3.4 dynamic_update_slice.8
  192.0 3.4 dynamic_update_slice.8
  201.7 3.4 dynamic_update_slice.8
  211.5 3.4 dynamic_update_slice.8
  218.7 6.0 collective-permute-start.5
  224.7 17.4 %collective-permute-done.4 = f32[6,2,64,256]{3,2,1,0:T(8,128)S(1)} collective-permute-done((f32[6,2,64,256]{3,2,1,0:T(8,128)S(1)}, f32[6,2,64,256]{3,2,1,0:T(8,128)S(1)}, u32[]{:S(2)}, u32[]{:S(2)}) %collective-permute-start.4) | collective-permute-done | bytes 786464 | tf_op jit(solution)/shard_map/ppermute | solution.py:23
  242.1 4.8 collective-permute-done.5
  249.2 3.0 fusion.370
  252.2 2.8 copy.198
  255.0 4.4 collective-permute-start.6
  259.4 2.8 copy.200
  280.6 3.5 scatter-add.35
  288.5 333.3 %all-gather.3.cloned.1.call-done = f32[512,128,128]{2,1,0:T(8,128)} async-done(((f32[2,128,128]{2,1,0:T(8,128)}), f32[512,128,128]{2,1,0:T(8,128)}) %all-gather.3.cloned.1.call-update) | async-done | bytes 33554448 | tf_op jit(solution)/shard_map/all_gather | solution.py:14
  621.8 12.2 %reduce_sum.29 = f32[2,128,128]{2,1,0:T(8,128)S(1)} reduce(f32[256,2,128,128]{3,2,1,0:T(8,128)} %bitcast.291, f32[]{:T(128)} %constant.275.clone.1), dimensions={0}, to_apply=%region_5.6 | reduce | flops 8355840 | bytes 33685508 | tf_op jit(solution)/shard_map/reduce_sum | solution.py:14
  (228 shorter events, 129.2 us)
Async XLA Ops:
  7.2 11.5 %copy-start.10 = (s32[1,8]{1,0:T(1,128)S(1)}, s32[1,8]{1,0:T(1,128)}, u32[]{:S(2)}) copy-start(s32[1,8]{1,0:T(1,128)} %param.27) | copy-start | bytes 100
  7.2 11.5 %copy-start.11 = (s32[1,8]{1,0:T(1,128)S(1)}, s32[1,8]{1,0:T(1,128)}, u32[]{:S(2)}) copy-start(s32[1,8]{1,0:T(1,128)} %param.28) | copy-start | bytes 100
  7.2 11.6 %copy-start.9 = (f32[2,128,128]{2,1,0:T(8,128)S(1)}, f32[2,128,128]{2,1,0:T(8,128)}, u32[]{:S(2)}) copy-start(f32[2,128,128]{2,1,0:T(8,128)} %param.25) | copy-start | bytes 393220
  7.2 614.6 %all-gather.3.cloned.1.call-start = ((), (), s32[]{:S(2)}) async-start(), calls=%async_computation | async-start | bytes 33685504 | tf_op jit(solution)/shard_map/all_gather | solution.py:14
  9.0 18.8 %collective-permute-start.1 = (f32[2,2,64,256]{2,3,1,0:T(8,128)S(1)}, f32[2,2,64,256]{2,3,1,0:T(8,128)S(1)}, u32[]{:S(2)}, u32[]{:S(2)}) collective-permute-start(f32[2,2,64,256]{2,3,1,0:T(8,128)S(1)} %get-tuple-element.281), channel_id=1, source_target_pairs={{16,0},{32,16},{48,32},{64,48},{80,64},{96,80},{112,96},{128,112},... | collective-permute-start | bytes 786440 | tf_op jit(solution)/shard_map/ppermute | solution.py:26
  16.7 17.6 %collective-permute-start = (f32[2,2,64,256]{2,3,1,0:T(8,128)S(1)}, f32[2,2,64,256]{2,3,1,0:T(8,128)S(1)}, u32[]{:S(2)}, u32[]{:S(2)}) collective-permute-start(f32[2,2,64,256]{2,3,1,0:T(8,128)S(1)} %get-tuple-element.280), channel_id=1, source_target_pairs={{0,16},{16,32},{32,48},{48,64},{64,80},{80,96},{96,112},{112,128},... | collective-permute-start | bytes 786440 | tf_op jit(solution)/shard_map/ppermute | solution.py:23
  27.9 6.5 %copy-start.1 = (f32[2,2,64,256]{2,3,1,0:T(8,128)}, f32[2,2,64,256]{2,3,1,0:T(8,128)S(1)}, u32[]{:S(2)}) copy-start(f32[2,2,64,256]{2,3,1,0:T(8,128)S(1)} %collective-permute-done.1) | copy-start | bytes 786436
  34.3 1.2 copy-start.3
  35.6 8.8 %collective-permute-start.3 = (f32[2,2,384,64]{2,3,1,0:T(8,128)}, f32[2,2,384,64]{2,3,1,0:T(8,128)}, u32[]{:S(2)}, u32[]{:S(2)}) collective-permute-start(f32[2,2,384,64]{2,3,1,0:T(8,128)} %get-tuple-element.265), channel_id=1, source_target_pairs={{1,0},{2,1},{3,2},{4,3},{5,4},{6,5},{7,6},{8,7},{9,8},{10,9},{11,1... | collective-permute-start | bytes 1179656 | tf_op jit(solution)/shard_map/ppermute | solution.py:26
  36.9 7.5 %collective-permute-start.2 = (f32[2,2,384,64]{2,3,1,0:T(8,128)}, f32[2,2,384,64]{2,3,1,0:T(8,128)}, u32[]{:S(2)}, u32[]{:S(2)}) collective-permute-start(f32[2,2,384,64]{2,3,1,0:T(8,128)} %get-tuple-element.264), channel_id=1, source_target_pairs={{0,1},{1,2},{2,3},{3,4},{4,5},{5,6},{6,7},{7,8},{8,9},{9,10},{10,1... | collective-permute-start | bytes 1179656 | tf_op jit(solution)/shard_map/ppermute | solution.py:23
  97.4 4.8 copy-start.4
  97.4 4.8 copy-start.13
  131.4 3.0 copy-start.2
  133.6 1.9 copy-start.5
  133.6 1.9 copy-start.6
  216.8 25.3 %collective-permute-start.4 = (f32[6,2,64,256]{3,2,1,0:T(8,128)S(1)}, f32[6,2,64,256]{3,2,1,0:T(8,128)S(1)}, u32[]{:S(2)}, u32[]{:S(2)}) collective-permute-start(f32[6,2,64,256]{3,2,1,0:T(8,128)S(1)} %get-tuple-element.251), channel_id=1, source_target_pairs={{0,16},{16,32},{32,48},{48,64},{64,80},{80,96},{96,112},{112,128},... | collective-permute-start | bytes 2359304 | tf_op jit(solution)/shard_map/ppermute | solution.py:23
  218.7 28.2 %collective-permute-start.5 = (f32[6,2,64,256]{3,2,1,0:T(8,128)S(1)}, f32[6,2,64,256]{3,2,1,0:T(8,128)S(1)}, u32[]{:S(2)}, u32[]{:S(2)}) collective-permute-start(f32[6,2,64,256]{3,2,1,0:T(8,128)S(1)} %get-tuple-element.250), channel_id=1, source_target_pairs={{16,0},{32,16},{48,32},{64,48},{80,64},{96,80},{112,96},{128,112},... | collective-permute-start | bytes 2359304 | tf_op jit(solution)/shard_map/ppermute | solution.py:26
  242.1 7.1 %copy-start.7 = (f32[6,2,64,256]{3,2,1,0:T(8,128)}, f32[6,2,64,256]{3,2,1,0:T(8,128)S(1)}, u32[]{:S(2)}) copy-start(f32[6,2,64,256]{3,2,1,0:T(8,128)S(1)} %collective-permute-done.4) | copy-start | bytes 2359300
  246.9 2.3 copy-start.8
  255.0 9.2 %copy-start.12 = (s32[4]{0:T(128)S(1)}, s32[4]{0:T(128)}, u32[]{:S(2)}) copy-start(s32[4]{0:T(128)} %constant.288.clone.1) | copy-start | bytes 52
  255.0 12.3 %collective-permute-start.6 = (f32[6,2,384,64]{2,3,1,0:T(8,128)}, f32[6,2,384,64]{2,3,1,0:T(8,128)}, u32[]{:S(2)}, u32[]{:S(2)}) collective-permute-start(f32[6,2,384,64]{2,3,1,0:T(8,128)} %copy.198), channel_id=1, source_target_pairs={{0,1},{1,2},{2,3},{3,4},{4,5},{5,6},{6,7},{7,8},{8,9},{9,10},{10,1... | collective-permute-start | bytes 3538952 | tf_op jit(solution)/shard_map/ppermute | solution.py:23
  262.2 8.8 %collective-permute-start.7 = (f32[6,2,384,64]{2,3,1,0:T(8,128)}, f32[6,2,384,64]{2,3,1,0:T(8,128)}, u32[]{:S(2)}, u32[]{:S(2)}) collective-permute-start(f32[6,2,384,64]{2,3,1,0:T(8,128)} %copy.200), channel_id=1, source_target_pairs={{1,0},{2,1},{3,2},{4,3},{5,4},{6,5},{7,6},{8,7},{9,8},{10,9},{11,1... | collective-permute-start | bytes 3538952 | tf_op jit(solution)/shard_map/ppermute | solution.py:26
  273.8 13.6 %copy-start = (f32[2,2,256,256]{3,2,1,0:T(8,128)S(1)}, f32[2,2,256,256]{3,2,1,0:T(8,128)}, u32[]{:S(2)}) copy-start(f32[2,2,256,256]{3,2,1,0:T(8,128)} %param.24) | copy-start | bytes 3145732
Sparse Core Ops, SparseCore 0:
  134.6 487.1 all-gather.2
